TPU v7x, 32 devices: a whole 2x2x4 slice. The times are simulated.
32 devices in a mesh: group: 4 (over x, core), ctx: 8 (over z, y).
Axes of the slice: x: 2, y: 2, z: 4, core: 2. Of those that a mesh axis runs over, the one named last changes fastest.
Arguments:
- query_rows: bfloat16 [4, 2048, 4096], P('group', 'ctx'), may hold values from -250 to 250
- key_rows: bfloat16 [4, 2048, 512], P('group', 'ctx'), may hold values from -7 to 7
- value_rows: bfloat16 [4, 2048, 512], P('group', 'ctx'), may hold values from -6 to 6
- documents: int32 [4, 2048], P('group', 'ctx'), may hold values from 0 to 3, never falling along the last dimension, each value on 1 to 1280 neighbouring positions
- owners: int32 [4, 64, 1], P('group', 'ctx'), may hold values from 0 to 3; in each aligned block of 8 rows (0 to 7, 8 to 15, ..., all dimensions but the last counted through in order) at most 2 rows name the same one
Outputs:
- attended: bfloat16 [4, 2048, 4096], P('group', 'ctx')
- page_pool: bfloat16 [4, 64, 2, 128, 128], P('group', 'ctx')
- page_scales: bfloat16 [4, 64, 2], P('group', 'ctx')
Inputs may be any that keep to these rules, and one draw needn't show every extreme that they name: `documents`: document numbers never fall along a group's tokens; each document has at most 1280 tokens. `owners`: among the pages of one device, no owner is named more than 2 times.
All inputs are finite; a program needn't handle non-finite values.
Results may differ from a plain program's by a relative error of at most 0.0028.
Values may be sent and summed in bfloat16 or wider, within the bound.
A program may use at most 128 MiB of HBM per device.

v0:
```python
import math
import jax
import jax.numpy as jnp
from jax import lax
from jax.sharding import PartitionSpec as P

E = 128
HQ = 32
HK = 4
PAGE = 128
epsilon = 1e-06
masked_score = -1e30


def split_heads(queries_here, keys_here, values_here, doc_marks):
    tokens = queries_here.shape[0]
    ctx_count = lax.axis_size("ctx")
    per_device = HQ // ctx_count
    score_scale = 1.0 / math.sqrt(E)
    kv_pairs = jnp.stack(
        [keys_here.reshape(tokens, HK, E), values_here.reshape(tokens, HK, E)], axis=2
    )
    spread = jnp.repeat(kv_pairs, ctx_count // HK, axis=1)
    spread_marks = jnp.broadcast_to(doc_marks[:, None], (tokens, ctx_count))
    all_pairs, all_marks = (
        lax.all_to_all(spread, "ctx", split_axis=1, concat_axis=0, tiled=True),
        lax.all_to_all(spread_marks, "ctx", split_axis=1, concat_axis=0, tiled=True),
    )
    key_all = all_pairs[:, 0, 0]
    value_all = all_pairs[:, 0, 1]
    marks_all = all_marks[:, 0]
    length = key_all.shape[0]
    key_pos = jnp.arange(length, dtype=jnp.int32)
    block_rows = math.gcd(length, 512)
    shaped = queries_here.reshape(tokens, ctx_count, per_device, E)
    head_rows = lax.all_to_all(shaped, "ctx", split_axis=1, concat_axis=0, tiled=True)[:, 0]
    head_count = head_rows.shape[1]

    def one_block(block_index):
        first_row = block_index * block_rows
        query_block = lax.dynamic_slice_in_dim(head_rows, first_row, block_rows, 0)
        mark_rows = lax.dynamic_slice_in_dim(marks_all, first_row, block_rows, 0)
        query_pos = first_row + jnp.arange(block_rows, dtype=jnp.int32)
        scores = (
            jnp.einsum("qhe,ke->hqk", query_block, key_all, preferred_element_type=jnp.float32)
            * score_scale
        )
        visible = (mark_rows[:, None] == marks_all[None, :]) & (
            query_pos[:, None] >= key_pos[None, :]
        )
        scores = jnp.where(visible, scores, masked_score)
        largest = jnp.max(scores, axis=-1, keepdims=True)
        weights = jnp.exp(scores - largest)
        totals = jnp.sum(weights, axis=-1)
        weighted = jnp.einsum(
            "hqk,ke->qhe",
            weights.astype(jnp.bfloat16),
            value_all,
            preferred_element_type=jnp.float32,
        )
        return (weighted / jnp.transpose(totals)[..., None]).astype(jnp.bfloat16)

    blocks = lax.map(one_block, jnp.arange(length // block_rows, dtype=jnp.int32))
    result = blocks.reshape(length, 1, head_count, E)
    merged = lax.all_to_all(result, "ctx", split_axis=0, concat_axis=1, tiled=True)
    return merged.reshape(tokens, HQ * E)


def deliver_pages(keys_here, values_here, owner_list):
    tokens = keys_here.shape[0]
    block_count = tokens // PAGE
    key_pages = keys_here.reshape(block_count, PAGE, HK, E).transpose(0, 2, 1, 3)
    value_pages = values_here.reshape(block_count, PAGE, HK, E).transpose(0, 2, 1, 3)
    page_count = block_count * HK
    kv_pairs = jnp.stack([key_pages, value_pages], axis=2).reshape(page_count, 2, PAGE, E)
    magnitude = jnp.max(jnp.abs(kv_pairs.astype(jnp.float32)), axis=(2, 3)) + epsilon
    scales = magnitude.astype(jnp.bfloat16)
    stored = (kv_pairs.astype(jnp.float32) / scales.astype(jnp.float32)[:, :, None, None]).astype(
        jnp.bfloat16
    )
    groups_n = lax.axis_size("group")
    slot_depth = max(2, (page_count + groups_n - 1) // groups_n)
    page_order = jnp.arange(page_count, dtype=jnp.int32)
    earlier = (owner_list[:, None] == owner_list[None, :]) & (
        page_order[None, :] < page_order[:, None]
    )
    page_rank = jnp.sum(earlier.astype(jnp.int32), axis=1)
    slot_of = owner_list * slot_depth + page_rank
    select = (
        jnp.arange(groups_n * slot_depth, dtype=jnp.int32)[:, None] == slot_of[None, :]
    ).astype(jnp.bfloat16)
    packed = jnp.dot(
        select, stored.reshape(page_count, 2 * PAGE * E), preferred_element_type=jnp.float32
    ).astype(jnp.bfloat16)
    packed_scales = jnp.dot(select, scales, preferred_element_type=jnp.float32).astype(jnp.bfloat16)
    packed = packed.reshape(groups_n, slot_depth, 2, PAGE, E)
    packed_scales = packed_scales.reshape(groups_n, slot_depth, 2)
    arrived, arrived_scales = (
        lax.all_to_all(packed, "group", split_axis=0, concat_axis=0, tiled=True),
        lax.all_to_all(packed_scales, "group", split_axis=0, concat_axis=0, tiled=True),
    )
    return (
        arrived.reshape(1, groups_n * slot_depth, 2, PAGE, E),
        arrived_scales.reshape(1, groups_n * slot_depth, 2),
    )


def local(query_rows, key_rows, value_rows, documents, owners):
    queries_here = query_rows[0]
    keys_here = key_rows[0]
    values_here = value_rows[0]
    doc_marks = documents[0].astype(jnp.bfloat16)
    attended = split_heads(queries_here, keys_here, values_here, doc_marks)
    page_pool, page_scales = deliver_pages(keys_here, values_here, owners[0, :, 0])
    return (attended[None], page_pool, page_scales)


def solution(mesh):
    placed = (
        P("group", "ctx", None),
        P("group", "ctx", None),
        P("group", "ctx", None),
        P("group", "ctx"),
        P("group", "ctx", None),
    )
    return jax.shard_map(
        local,
        mesh=mesh,
        in_specs=placed,
        out_specs=(
            P("group", "ctx", None),
            P("group", "ctx", None, None, None),
            P("group", "ctx", None),
        ),
        check_vma=False,
    )
```

profile of v0, /device:TPU:0, one launch (start us, length us, event | category | flops | bytes accessed | tf_op | source)
XLA Modules:
  0.0 243.0 jit_solution(9955925464402207372)
XLA Ops:
  3.1 7.3 %all-to-all-start = ((bf16[8,2,128]{2,1,0:T(2,128)(2,1)}), bf16[8,2,128]{2,1,0:T(2,128)(2,1)S(1)}, u32[]{:S(2)}, u32[]{:S(2)}) async-start(bf16[8,2,128]{2,1,0:T(2,128)(2,1)} %reshape.89), calls=%async_computation | async-start | bytes 8192 | tf_op jit(solution)/shard_map/all_to_all | solution.py:27
  12.9 3.9 %all-to-all-done = bf16[8,2,128]{2,1,0:T(2,128)(2,1)S(1)} async-done(((bf16[8,2,128]{2,1,0:T(2,128)(2,1)}), bf16[8,2,128]{2,1,0:T(2,128)(2,1)S(1)}, u32[]{:S(2)}, u32[]{:S(2)}) %all-to-all-start) | async-done | bytes 4128 | tf_op jit(solution)/shard_map/all_to_all | solution.py:27
  18.0 3.6 %all-to-all-start.2 = ((bf16[256,8,2,128]{3,0,2,1:T(8,128)(2,1)}), bf16[256,8,2,128]{3,0,2,1:T(8,128)(2,1)S(1)}, u32[]{:S(2)}, u32[]{:S(2)}) async-start(bf16[256,8,2,128]{3,0,2,1:T(8,128)(2,1)} %bitcast.6), calls=%async_computation.2 | async-start | bytes 2097152 | tf_op jit(solution)/shard_map/all_to_all | solution.py:26
  21.6 3.3 %copy.47 = bf16[1,256,4096]{1,2,0:T(8,128)(2,1)S(1)} copy(bf16[1,256,4096]{2,1,0:T(8,128)(2,1)} %param.7) | data formatting | bytes 4194304 | tf_op args[0]
  27.3 19.0 %all-to-all-done.2 = bf16[256,8,2,128]{3,0,2,1:T(8,128)(2,1)S(1)} async-done(((bf16[256,8,2,128]{3,0,2,1:T(8,128)(2,1)}), bf16[256,8,2,128]{3,0,2,1:T(8,128)(2,1)S(1)}, u32[]{:S(2)}, u32[]{:S(2)}) %all-to-all-start.2) | async-done | bytes 1048608 | tf_op jit(solution)/shard_map/all_to_all | solution.py:26
  46.3 3.6 %all-to-all-start.1 = ((bf16[256,8,4,128]{3,0,2,1:T(8,128)(2,1)}), bf16[256,8,4,128]{3,0,2,1:T(8,128)(2,1)S(1)}, u32[]{:S(2)}, u32[]{:S(2)}) async-start(bf16[256,8,4,128]{3,0,2,1:T(8,128)(2,1)} %copy.48), calls=%async_computation.1 | async-start | bytes 4194304 | tf_op jit(solution)/shard_map/all_to_all | solution.py:36
  56.6 41.6 %all-to-all-done.1 = bf16[256,8,4,128]{3,0,2,1:T(8,128)(2,1)S(1)} async-done(((bf16[256,8,4,128]{3,0,2,1:T(8,128)(2,1)}), bf16[256,8,4,128]{3,0,2,1:T(8,128)(2,1)S(1)}, u32[]{:S(2)}, u32[]{:S(2)}) %all-to-all-start.1) | async-done | bytes 2097184 | tf_op jit(solution)/shard_map/all_to_all | solution.py:36
  105.1 3.5 %all-to-all-start.4 = ((bf16[4,2,2,128,128]{4,3,2,1,0:T(8,128)(2,1)}), bf16[4,2,2,128,128]{4,3,2,1,0:T(8,128)(2,1)S(1)}, u32[]{:S(2)}, u32[]{:S(2)}) async-start(bf16[4,2,2,128,128]{4,3,2,1,0:T(8,128)(2,1)} %bitcast.44), calls=%async_computation.4 | async-start | bytes 1048576 | tf_op jit(solution)/shard_map/all_to_all | solution.py:99
  108.6 68.9 %while.11 = (s32[]{:T(128)}, bf16[4,512,4,128]{3,1,0,2:T(8,128)(2,1)}, s32[4]{0:T(128)S(1)}, bf16[2048]{0:T(1024)(128)(2,1)S(1)}, bf16[2048,1]{0,1:T(2,128)(2,1)...) while((s32[]{:T(128)}, ...), condition=%wide.region_3.4_spmd.clone, body=%wide.region_0.3_spmd.clone.sunk | while | flops 2199384576 | bytes 56683728 | solution.py:63
  111.2 4.8 %bitcast_reduce_fusion.3 = (f32[4,512]{1,0:T(4,128)S(1)}, f32[512,4,2048]{2,0,1:T(8,128)S(1)}) fusion(pred[512,2048]{1,0:T(8,128)(4,1)S(1)} %fusion.44, bf16[2048,128]{1,0:T(8,128)(2,1)} %get-tuple-element.186, bf16[2048,4,128]{2,0,1:T(8,128)(2,1)} %get-tuple-element.185, s32[]{:T(128)S(6)} %select_n.39), kind=kOutput, calls=%fused_computation.2.clone.1 | convolution fusion | flops 1086322688 | bytes 18882564 | tf_op jit(solution)/shard_map/while/body/eval_jaxpr/qhe,ke->hqk/dot_general | solution.py:45
  115.9 4.5 %fusion.45 = f32[4,512]{1,0:T(4,128)S(1)} fusion(f32[512,4,2048]{2,0,1:T(8,128)S(1)} %get-tuple-element.152, f32[4,512]{1,0:T(4,128)S(1)} %get-tuple-element.153, pred[512,2048]{1,0:T(8,128)(4,1)S(1)} %fusion.44), kind=kLoop, calls=%fused_computation.5.clone.1 | loop fusion | flops 16775168 | bytes 17842176 | tf_op jit(solution)/shard_map/while/body/eval_jaxpr/reduce_sum | solution.py:54
  120.4 5.4 %fusion.46 = bf16[4,512,4,128]{3,1,0,2:T(8,128)(2,1)} fusion(bf16[4,512,4,128]{3,1,0,2:T(8,128)(2,1)} %get-tuple-element.168, s32[]{:T(128)S(6)} %copy.74, f32[512,4,2048]{2,0,1:T(8,128)S(1)} %get-tuple-element.152, f32[4,512]{1,0:T(4,128)S(1)} %get-tuple-element.153, pred[512,2048]{1,0:T(8,128)(4,1)S(1)} %fusion.44, ...), kind=kOutput, calls=%fused_computation.14.clone.1 | convolution fusion | flops 1091043328 | bytes 18890756 | tf_op jit(solution)/shard_map/while/body/eval_jaxpr/hqk,ke->qhe/dot_general | solution.py:55
  128.4 4.8 %bitcast_reduce_fusion.3 = (f32[4,512]{1,0:T(4,128)S(1)}, f32[512,4,2048]{2,0,1:T(8,128)S(1)}) fusion(pred[512,2048]{1,0:T(8,128)(4,1)S(1)} %fusion.44, bf16[2048,128]{1,0:T(8,128)(2,1)} %get-tuple-element.186, bf16[2048,4,128]{2,0,1:T(8,128)(2,1)} %get-tuple-element.185, s32[]{:T(128)S(6)} %select_n.39), kind=kOutput, calls=%fused_computation.2.clone.1 | convolution fusion | flops 1086322688 | bytes 18882564 | tf_op jit(solution)/shard_map/while/body/eval_jaxpr/qhe,ke->hqk/dot_general | solution.py:45
  133.1 4.5 %fusion.45 = f32[4,512]{1,0:T(4,128)S(1)} fusion(f32[512,4,2048]{2,0,1:T(8,128)S(1)} %get-tuple-element.152, f32[4,512]{1,0:T(4,128)S(1)} %get-tuple-element.153, pred[512,2048]{1,0:T(8,128)(4,1)S(1)} %fusion.44), kind=kLoop, calls=%fused_computation.5.clone.1 | loop fusion | flops 16775168 | bytes 17842176 | tf_op jit(solution)/shard_map/while/body/eval_jaxpr/reduce_sum | solution.py:54
  137.6 5.4 %fusion.46 = bf16[4,512,4,128]{3,1,0,2:T(8,128)(2,1)} fusion(bf16[4,512,4,128]{3,1,0,2:T(8,128)(2,1)} %get-tuple-element.168, s32[]{:T(128)S(6)} %copy.74, f32[512,4,2048]{2,0,1:T(8,128)S(1)} %get-tuple-element.152, f32[4,512]{1,0:T(4,128)S(1)} %get-tuple-element.153, pred[512,2048]{1,0:T(8,128)(4,1)S(1)} %fusion.44, ...), kind=kOutput, calls=%fused_computation.14.clone.1 | convolution fusion | flops 1091043328 | bytes 18890756 | tf_op jit(solution)/shard_map/while/body/eval_jaxpr/hqk,ke->qhe/dot_general | solution.py:55
  145.6 4.8 %bitcast_reduce_fusion.3 = (f32[4,512]{1,0:T(4,128)S(1)}, f32[512,4,2048]{2,0,1:T(8,128)S(1)}) fusion(pred[512,2048]{1,0:T(8,128)(4,1)S(1)} %fusion.44, bf16[2048,128]{1,0:T(8,128)(2,1)} %get-tuple-element.186, bf16[2048,4,128]{2,0,1:T(8,128)(2,1)} %get-tuple-element.185, s32[]{:T(128)S(6)} %select_n.39), kind=kOutput, calls=%fused_computation.2.clone.1 | convolution fusion | flops 1086322688 | bytes 18882564 | tf_op jit(solution)/shard_map/while/body/eval_jaxpr/qhe,ke->hqk/dot_general | solution.py:45
  150.4 4.5 %fusion.45 = f32[4,512]{1,0:T(4,128)S(1)} fusion(f32[512,4,2048]{2,0,1:T(8,128)S(1)} %get-tuple-element.152, f32[4,512]{1,0:T(4,128)S(1)} %get-tuple-element.153, pred[512,2048]{1,0:T(8,128)(4,1)S(1)} %fusion.44), kind=kLoop, calls=%fused_computation.5.clone.1 | loop fusion | flops 16775168 | bytes 17842176 | tf_op jit(solution)/shard_map/while/body/eval_jaxpr/reduce_sum | solution.py:54
  154.8 5.4 %fusion.46 = bf16[4,512,4,128]{3,1,0,2:T(8,128)(2,1)} fusion(bf16[4,512,4,128]{3,1,0,2:T(8,128)(2,1)} %get-tuple-element.168, s32[]{:T(128)S(6)} %copy.74, f32[512,4,2048]{2,0,1:T(8,128)S(1)} %get-tuple-element.152, f32[4,512]{1,0:T(4,128)S(1)} %get-tuple-element.153, pred[512,2048]{1,0:T(8,128)(4,1)S(1)} %fusion.44, ...), kind=kOutput, calls=%fused_computation.14.clone.1 | convolution fusion | flops 1091043328 | bytes 18890756 | tf_op jit(solution)/shard_map/while/body/eval_jaxpr/hqk,ke->qhe/dot_general | solution.py:55
  162.8 4.8 %bitcast_reduce_fusion.3 = (f32[4,512]{1,0:T(4,128)S(1)}, f32[512,4,2048]{2,0,1:T(8,128)S(1)}) fusion(pred[512,2048]{1,0:T(8,128)(4,1)S(1)} %fusion.44, bf16[2048,128]{1,0:T(8,128)(2,1)} %get-tuple-element.186, bf16[2048,4,128]{2,0,1:T(8,128)(2,1)} %get-tuple-element.185, s32[]{:T(128)S(6)} %select_n.39), kind=kOutput, calls=%fused_computation.2.clone.1 | convolution fusion | flops 1086322688 | bytes 18882564 | tf_op jit(solution)/shard_map/while/body/eval_jaxpr/qhe,ke->hqk/dot_general | solution.py:45
  167.6 4.5 %fusion.45 = f32[4,512]{1,0:T(4,128)S(1)} fusion(f32[512,4,2048]{2,0,1:T(8,128)S(1)} %get-tuple-element.152, f32[4,512]{1,0:T(4,128)S(1)} %get-tuple-element.153, pred[512,2048]{1,0:T(8,128)(4,1)S(1)} %fusion.44), kind=kLoop, calls=%fused_computation.5.clone.1 | loop fusion | flops 16775168 | bytes 17842176 | tf_op jit(solution)/shard_map/while/body/eval_jaxpr/reduce_sum | solution.py:54
  172.1 5.4 %fusion.46 = bf16[4,512,4,128]{3,1,0,2:T(8,128)(2,1)} fusion(bf16[4,512,4,128]{3,1,0,2:T(8,128)(2,1)} %get-tuple-element.168, s32[]{:T(128)S(6)} %copy.74, f32[512,4,2048]{2,0,1:T(8,128)S(1)} %get-tuple-element.152, f32[4,512]{1,0:T(4,128)S(1)} %get-tuple-element.153, pred[512,2048]{1,0:T(8,128)(4,1)S(1)} %fusion.44, ...), kind=kOutput, calls=%fused_computation.14.clone.1 | convolution fusion | flops 1091043328 | bytes 18890756 | tf_op jit(solution)/shard_map/while/body/eval_jaxpr/hqk,ke->qhe/dot_general | solution.py:55
  177.5 4.7 %copy.53 = bf16[2048,1,4,128]{3,2,1,0:T(4,128)(2,1)} copy(bf16[2048,1,4,128]{3,0,2,1:T(8,128)(2,1)} %bitcast.120) | data formatting | bytes 4194304 | tf_op jit(solution)/shard_map/reshape | solution.py:64
  182.2 3.6 %all-to-all-start.3 = ((bf16[2048,1,4,128]{3,2,1,0:T(4,128)(2,1)}), bf16[2048,1,4,128]{3,2,1,0:T(4,128)(2,1)S(1)}, u32[]{:S(2)}, u32[]{:S(2)}) async-start(bf16[2048,1,4,128]{3,2,1,0:T(4,128)(2,1)} %copy.53), calls=%async_computation.3 | async-start | bytes 4194304 | tf_op jit(solution)/shard_map/all_to_all | solution.py:65
  186.4 48.4 %all-to-all-done.3 = bf16[2048,1,4,128]{3,2,1,0:T(4,128)(2,1)S(1)} async-done(((bf16[2048,1,4,128]{3,2,1,0:T(4,128)(2,1)}), bf16[2048,1,4,128]{3,2,1,0:T(4,128)(2,1)S(1)}, u32[]{:S(2)}, u32[]{:S(2)}) %all-to-all-start.3) | async-done | bytes 2097184 | tf_op jit(solution)/shard_map/all_to_all | solution.py:65
  (67 shorter events, 38.3 us)
Async XLA Ops:
  3.1 13.7 %all-to-all-start = ((bf16[8,2,128]{2,1,0:T(2,128)(2,1)}), bf16[8,2,128]{2,1,0:T(2,128)(2,1)S(1)}, u32[]{:S(2)}, u32[]{:S(2)}) async-start(bf16[8,2,128]{2,1,0:T(2,128)(2,1)} %reshape.89), calls=%async_computation | async-start | bytes 8192 | tf_op jit(solution)/shard_map/all_to_all | solution.py:27
  18.0 28.3 %all-to-all-start.2 = ((bf16[256,8,2,128]{3,0,2,1:T(8,128)(2,1)}), bf16[256,8,2,128]{3,0,2,1:T(8,128)(2,1)S(1)}, u32[]{:S(2)}, u32[]{:S(2)}) async-start(bf16[256,8,2,128]{3,0,2,1:T(8,128)(2,1)} %bitcast.6), calls=%async_computation.2 | async-start | bytes 2097152 | tf_op jit(solution)/shard_map/all_to_all | solution.py:26
  24.9 25.1 %copy-start = (bf16[1,256,512]{2,1,0:T(8,128)(2,1)S(1)}, bf16[1,256,512]{2,1,0:T(8,128)(2,1)}, u32[]{:S(2)}) copy-start(bf16[1,256,512]{2,1,0:T(8,128)(2,1)} %param.9) | copy-start | bytes 786436
  27.3 26.0 %copy-start.1 = (s32[1,8,1]{1,2,0:T(1,128)S(1)}, s32[1,8,1]{1,2,0:T(1,128)}, u32[]{:S(2)}) copy-start(s32[1,8,1]{1,2,0:T(1,128)} %param.11) | copy-start | bytes 100
  46.3 51.9 %all-to-all-start.1 = ((bf16[256,8,4,128]{3,0,2,1:T(8,128)(2,1)}), bf16[256,8,4,128]{3,0,2,1:T(8,128)(2,1)S(1)}, u32[]{:S(2)}, u32[]{:S(2)}) async-start(bf16[256,8,4,128]{3,0,2,1:T(8,128)(2,1)} %copy.48), calls=%async_computation.1 | async-start | bytes 4194304 | tf_op jit(solution)/shard_map/all_to_all | solution.py:36
  98.2 6.9 %all-to-all-start.5 = ((bf16[4,2,2]{1,2,0:T(2,128)(2,1)}), bf16[4,2,2]{1,2,0:T(2,128)(2,1)S(1)}, u32[]{:S(2)}, u32[]{:S(2)}) async-start(bf16[4,2,2]{1,2,0:T(2,128)(2,1)} %copy.59), calls=%async_computation.5 | async-start | bytes 4096 | tf_op jit(solution)/shard_map/all_to_all | solution.py:100
  105.1 77.1 %all-to-all-start.4 = ((bf16[4,2,2,128,128]{4,3,2,1,0:T(8,128)(2,1)}), bf16[4,2,2,128,128]{4,3,2,1,0:T(8,128)(2,1)S(1)}, u32[]{:S(2)}, u32[]{:S(2)}) async-start(bf16[4,2,2,128,128]{4,3,2,1,0:T(8,128)(2,1)} %bitcast.44), calls=%async_computation.4 | async-start | bytes 1048576 | tf_op jit(solution)/shard_map/all_to_all | solution.py:99
  182.2 52.7 %all-to-all-start.3 = ((bf16[2048,1,4,128]{3,2,1,0:T(4,128)(2,1)}), bf16[2048,1,4,128]{3,2,1,0:T(4,128)(2,1)S(1)}, u32[]{:S(2)}, u32[]{:S(2)}) async-start(bf16[2048,1,4,128]{3,2,1,0:T(4,128)(2,1)} %copy.53), calls=%async_computation.3 | async-start | bytes 4194304 | tf_op jit(solution)/shard_map/all_to_all | solution.py:65
where the time goes:
time: 244 us; the launch traced here: 243 us
  waiting for transfers between devices  115 us (47%)
  matrix products  41.3 us (17%)
  local copies, waits for them, and re-layouts  33.1 us (14%)
  other arithmetic  25.2 us (10%)
  starting transfers between devices  24.7 us (10%)
  loops' own time  2.64 us (1%)
    all_to_all x1, waiting for transfers between devices, split_heads(): lax.all_to_all(result, 'ctx', split_axis=0, concat_axis=1, tiled=True)  48.4 us
    all_to_all x1, waiting for transfers between devices, split_heads(): lax.all_to_all(shaped, 'ctx', split_axis=1, concat_axis=0, tiled=True)[:, 0]  41.6 us
    dot_general x4, matrix products, one_block(): jnp.einsum('hqk,ke->qhe', weights.astype(jnp.bfloat16), value_all, prefer...  21.7 us
    dot_general x4, matrix products, one_block(): jnp.einsum('qhe,ke->hqk', query_block, key_all, preferred_element_type=jn...  19 us
    all_to_all x1, waiting for transfers between devices, split_heads(): lax.all_to_all(spread, 'ctx', split_axis=1, concat_axis=0, tiled=True)  19 us
    reduce_sum x4, other arithmetic, one_block(): totals = jnp.sum(weights, axis=-1)  17.9 us
    unnamed x13, local copies, waits for them, and re-layouts  8.97 us
    all_to_all x1, starting transfers between devices, split_heads(): lax.all_to_all(spread_marks, 'ctx', split_axis=1, concat_axis=0, tiled=True)  7.31 us
  transfers between devices with their start and end apart: 6, of which 5 were waited for; matrix products, arithmetic and copies ran while one was open for 36% of the time, Pallas kernels for 0%

commit v1 on v0

--- a/solution.py
+++ b/solution.py
@@ -62,7 +62,10 @@
 
     blocks = lax.map(one_block, jnp.arange(length // block_rows, dtype=jnp.int32))
     result = blocks.reshape(length, 1, head_count, E)
-    merged = lax.all_to_all(result, "ctx", split_axis=0, concat_axis=1, tiled=True)
+    merged = jnp.concatenate(
+        lax.all_to_all(jnp.stack(jnp.split(result, lax.axis_size("ctx"), axis=0)), "ctx", 0, 0),
+        axis=1,
+    )
     return merged.reshape(tokens, HQ * E)
 
 

time: 244 us -> 250 us (1.025)
  local copies, waits for them, and re-layouts: 33.1 us -> 36.3 us
  waiting for transfers between devices: 115 us -> 118 us
    unnamed x13 -> x22, local copies, waits for them, and re-layouts: 8.97 us -> 18.4 us
    all_to_all x1, waiting for transfers between devices: 0.01 us -> 5.47 us  [deliver_pages(): lax.all_to_all(packed, 'group', split_axis=0, concat_axis=0, tiled=True)]
    all_to_all x2 -> x0, local copies, waits for them, and re-layouts: 4.45 us -> none  [split_heads(): lax.all_to_all(result, 'ctx', split_axis=0, concat_axis=1, tiled=True)]
where the time goes in v1:
time: 250 us; the launch traced here: 248 us
  waiting for transfers between devices  118 us (47%)
  matrix products  40.5 us (16%)
  local copies, waits for them, and re-layouts  36.3 us (15%)
  other arithmetic  25.2 us (10%)
  starting transfers between devices  24.7 us (10%)
  loops' own time  2.55 us (1%)
    all_to_all x1, waiting for transfers between devices, split_heads(): lax.all_to_all(jnp.stack(jnp.split(result, lax.axis_size('ctx'), axis=0))...  47.5 us
    all_to_all x1, waiting for transfers between devices, split_heads(): lax.all_to_all(shaped, 'ctx', split_axis=1, concat_axis=0, tiled=True)[:, 0]  42.4 us
    dot_general x4, matrix products, one_block(): jnp.einsum('hqk,ke->qhe', weights.astype(jnp.bfloat16), value_all, prefer...  21.7 us
    all_to_all x1, waiting for transfers between devices, split_heads(): lax.all_to_all(spread, 'ctx', split_axis=1, concat_axis=0, tiled=True)  19 us
    unnamed x22, local copies, waits for them, and re-layouts  18.4 us
    dot_general x4, matrix products, one_block(): jnp.einsum('qhe,ke->hqk', query_block, key_all, preferred_element_type=jn...  18.3 us
    reduce_sum x4, other arithmetic, one_block(): totals = jnp.sum(weights, axis=-1)  17.9 us
    all_to_all x1, starting transfers between devices, split_heads(): lax.all_to_all(spread_marks, 'ctx', split_axis=1, concat_axis=0, tiled=True)  7.31 us
  transfers between devices with their start and end apart: 6, of which 5 were waited for; matrix products, arithmetic and copies ran while one was open for 36% of the time, Pallas kernels for 0%

profile of v1, /device:TPU:0, one launch (start us, length us, event | category | flops | bytes accessed | tf_op | source)
XLA Modules:
  0.0 248.5 jit_solution(6279608549576770718)
XLA Ops:
  3.1 7.3 %all-to-all-start = ((bf16[8,2,128]{2,1,0:T(2,128)(2,1)}), bf16[8,2,128]{2,1,0:T(2,128)(2,1)S(1)}, u32[]{:S(2)}, u32[]{:S(2)}) async-start(bf16[8,2,128]{2,1,0:T(2,128)(2,1)} %reshape.92), calls=%async_computation | async-start | bytes 8192 | tf_op jit(solution)/shard_map/all_to_all | solution.py:27
  12.9 3.9 %all-to-all-done = bf16[8,2,128]{2,1,0:T(2,128)(2,1)S(1)} async-done(((bf16[8,2,128]{2,1,0:T(2,128)(2,1)}), bf16[8,2,128]{2,1,0:T(2,128)(2,1)S(1)}, u32[]{:S(2)}, u32[]{:S(2)}) %all-to-all-start) | async-done | bytes 4128 | tf_op jit(solution)/shard_map/all_to_all | solution.py:27
  18.0 3.6 %all-to-all-start.2 = ((bf16[256,8,2,128]{3,0,2,1:T(8,128)(2,1)}), bf16[256,8,2,128]{3,0,2,1:T(8,128)(2,1)S(1)}, u32[]{:S(2)}, u32[]{:S(2)}) async-start(bf16[256,8,2,128]{3,0,2,1:T(8,128)(2,1)} %bitcast.6), calls=%async_computation.2 | async-start | bytes 2097152 | tf_op jit(solution)/shard_map/all_to_all | solution.py:26
  27.3 19.0 %all-to-all-done.2 = bf16[256,8,2,128]{3,0,2,1:T(8,128)(2,1)S(1)} async-done(((bf16[256,8,2,128]{3,0,2,1:T(8,128)(2,1)}), bf16[256,8,2,128]{3,0,2,1:T(8,128)(2,1)S(1)}, u32[]{:S(2)}, u32[]{:S(2)}) %all-to-all-start.2) | async-done | bytes 1048608 | tf_op jit(solution)/shard_map/all_to_all | solution.py:26
  46.3 3.6 %all-to-all-start.1 = ((bf16[256,8,4,128]{3,0,2,1:T(8,128)(2,1)}), bf16[256,8,4,128]{3,0,2,1:T(8,128)(2,1)S(1)}, u32[]{:S(2)}, u32[]{:S(2)}) async-start(bf16[256,8,4,128]{3,0,2,1:T(8,128)(2,1)} %copy.51), calls=%async_computation.1 | async-start | bytes 4194304 | tf_op jit(solution)/shard_map/all_to_all | solution.py:36
  55.8 42.4 %all-to-all-done.1 = bf16[256,8,4,128]{3,0,2,1:T(8,128)(2,1)S(1)} async-done(((bf16[256,8,4,128]{3,0,2,1:T(8,128)(2,1)}), bf16[256,8,4,128]{3,0,2,1:T(8,128)(2,1)S(1)}, u32[]{:S(2)}, u32[]{:S(2)}) %all-to-all-start.1) | async-done | bytes 2097184 | tf_op jit(solution)/shard_map/all_to_all | solution.py:36
  102.9 68.2 %while.11 = (s32[]{:T(128)}, bf16[4,512,4,128]{3,1,0,2:T(8,128)(2,1)}, s32[4]{0:T(128)S(1)}, bf16[2048]{0:T(1024)(128)(2,1)S(1)}, bf16[2048,1]{0,1:T(2,128)(2,1)...) while((s32[]{:T(128)}, ...), condition=%wide.region_3.4_spmd.clone, body=%wide.region_0.3_spmd.clone.sunk | while | flops 2199384576 | bytes 56684228 | solution.py:63
  105.4 4.6 %bitcast_reduce_fusion.3 = (f32[4,512]{1,0:T(4,128)S(1)}, f32[512,4,2048]{2,0,1:T(8,128)S(1)}) fusion(pred[512,2048]{1,0:T(8,128)(4,1)S(1)} %fusion.52, bf16[2048,128]{1,0:T(8,128)(2,1)S(1)} %get-tuple-element.186, bf16[2048,4,128]{2,0,1:T(8,128)(2,1)} %get-tuple-element.185, s32[]{:T(128)S(6)} %select_n.39), kind=kOutput, calls=%fused_computation.2.clone.1 | convolution fusion | flops 1086322688 | bytes 18882564 | tf_op jit(solution)/shard_map/while/body/eval_jaxpr/qhe,ke->hqk/dot_general | solution.py:45
  110.0 4.5 %fusion.53 = f32[4,512]{1,0:T(4,128)S(1)} fusion(f32[512,4,2048]{2,0,1:T(8,128)S(1)} %get-tuple-element.152, f32[4,512]{1,0:T(4,128)S(1)} %get-tuple-element.153, pred[512,2048]{1,0:T(8,128)(4,1)S(1)} %fusion.52), kind=kLoop, calls=%fused_computation.5.clone.1 | loop fusion | flops 16775168 | bytes 17842176 | tf_op jit(solution)/shard_map/while/body/eval_jaxpr/reduce_sum | solution.py:54
  114.5 5.4 %fusion.54 = bf16[4,512,4,128]{3,1,0,2:T(8,128)(2,1)} fusion(bf16[4,512,4,128]{3,1,0,2:T(8,128)(2,1)} %get-tuple-element.168, s32[]{:T(128)} %get-tuple-element.167, f32[512,4,2048]{2,0,1:T(8,128)S(1)} %get-tuple-element.152, f32[4,512]{1,0:T(4,128)S(1)} %get-tuple-element.153, pred[512,2048]{1,0:T(8,128)(4,1)S(1)} %fusion.52, ...), kind=kOutput, calls=%fused_computation.14.clone.1 | convolution fusion | flops 1091043328 | bytes 18891264 | tf_op jit(solution)/shard_map/while/body/eval_jaxpr/hqk,ke->qhe/dot_general | solution.py:55
  122.5 4.6 %bitcast_reduce_fusion.3 = (f32[4,512]{1,0:T(4,128)S(1)}, f32[512,4,2048]{2,0,1:T(8,128)S(1)}) fusion(pred[512,2048]{1,0:T(8,128)(4,1)S(1)} %fusion.52, bf16[2048,128]{1,0:T(8,128)(2,1)S(1)} %get-tuple-element.186, bf16[2048,4,128]{2,0,1:T(8,128)(2,1)} %get-tuple-element.185, s32[]{:T(128)S(6)} %select_n.39), kind=kOutput, calls=%fused_computation.2.clone.1 | convolution fusion | flops 1086322688 | bytes 18882564 | tf_op jit(solution)/shard_map/while/body/eval_jaxpr/qhe,ke->hqk/dot_general | solution.py:45
  127.1 4.5 %fusion.53 = f32[4,512]{1,0:T(4,128)S(1)} fusion(f32[512,4,2048]{2,0,1:T(8,128)S(1)} %get-tuple-element.152, f32[4,512]{1,0:T(4,128)S(1)} %get-tuple-element.153, pred[512,2048]{1,0:T(8,128)(4,1)S(1)} %fusion.52), kind=kLoop, calls=%fused_computation.5.clone.1 | loop fusion | flops 16775168 | bytes 17842176 | tf_op jit(solution)/shard_map/while/body/eval_jaxpr/reduce_sum | solution.py:54
  131.5 5.4 %fusion.54 = bf16[4,512,4,128]{3,1,0,2:T(8,128)(2,1)} fusion(bf16[4,512,4,128]{3,1,0,2:T(8,128)(2,1)} %get-tuple-element.168, s32[]{:T(128)} %get-tuple-element.167, f32[512,4,2048]{2,0,1:T(8,128)S(1)} %get-tuple-element.152, f32[4,512]{1,0:T(4,128)S(1)} %get-tuple-element.153, pred[512,2048]{1,0:T(8,128)(4,1)S(1)} %fusion.52, ...), kind=kOutput, calls=%fused_computation.14.clone.1 | convolution fusion | flops 1091043328 | bytes 18891264 | tf_op jit(solution)/shard_map/while/body/eval_jaxpr/hqk,ke->qhe/dot_general | solution.py:55
  139.5 4.6 %bitcast_reduce_fusion.3 = (f32[4,512]{1,0:T(4,128)S(1)}, f32[512,4,2048]{2,0,1:T(8,128)S(1)}) fusion(pred[512,2048]{1,0:T(8,128)(4,1)S(1)} %fusion.52, bf16[2048,128]{1,0:T(8,128)(2,1)S(1)} %get-tuple-element.186, bf16[2048,4,128]{2,0,1:T(8,128)(2,1)} %get-tuple-element.185, s32[]{:T(128)S(6)} %select_n.39), kind=kOutput, calls=%fused_computation.2.clone.1 | convolution fusion | flops 1086322688 | bytes 18882564 | tf_op jit(solution)/shard_map/while/body/eval_jaxpr/qhe,ke->hqk/dot_general | solution.py:45
  144.1 4.5 %fusion.53 = f32[4,512]{1,0:T(4,128)S(1)} fusion(f32[512,4,2048]{2,0,1:T(8,128)S(1)} %get-tuple-element.152, f32[4,512]{1,0:T(4,128)S(1)} %get-tuple-element.153, pred[512,2048]{1,0:T(8,128)(4,1)S(1)} %fusion.52), kind=kLoop, calls=%fused_computation.5.clone.1 | loop fusion | flops 16775168 | bytes 17842176 | tf_op jit(solution)/shard_map/while/body/eval_jaxpr/reduce_sum | solution.py:54
  148.6 5.4 %fusion.54 = bf16[4,512,4,128]{3,1,0,2:T(8,128)(2,1)} fusion(bf16[4,512,4,128]{3,1,0,2:T(8,128)(2,1)} %get-tuple-element.168, s32[]{:T(128)} %get-tuple-element.167, f32[512,4,2048]{2,0,1:T(8,128)S(1)} %get-tuple-element.152, f32[4,512]{1,0:T(4,128)S(1)} %get-tuple-element.153, pred[512,2048]{1,0:T(8,128)(4,1)S(1)} %fusion.52, ...), kind=kOutput, calls=%fused_computation.14.clone.1 | convolution fusion | flops 1091043328 | bytes 18891264 | tf_op jit(solution)/shard_map/while/body/eval_jaxpr/hqk,ke->qhe/dot_general | solution.py:55
  156.6 4.6 %bitcast_reduce_fusion.3 = (f32[4,512]{1,0:T(4,128)S(1)}, f32[512,4,2048]{2,0,1:T(8,128)S(1)}) fusion(pred[512,2048]{1,0:T(8,128)(4,1)S(1)} %fusion.52, bf16[2048,128]{1,0:T(8,128)(2,1)S(1)} %get-tuple-element.186, bf16[2048,4,128]{2,0,1:T(8,128)(2,1)} %get-tuple-element.185, s32[]{:T(128)S(6)} %select_n.39), kind=kOutput, calls=%fused_computation.2.clone.1 | convolution fusion | flops 1086322688 | bytes 18882564 | tf_op jit(solution)/shard_map/while/body/eval_jaxpr/qhe,ke->hqk/dot_general | solution.py:45
  161.1 4.5 %fusion.53 = f32[4,512]{1,0:T(4,128)S(1)} fusion(f32[512,4,2048]{2,0,1:T(8,128)S(1)} %get-tuple-element.152, f32[4,512]{1,0:T(4,128)S(1)} %get-tuple-element.153, pred[512,2048]{1,0:T(8,128)(4,1)S(1)} %fusion.52), kind=kLoop, calls=%fused_computation.5.clone.1 | loop fusion | flops 16775168 | bytes 17842176 | tf_op jit(solution)/shard_map/while/body/eval_jaxpr/reduce_sum | solution.py:54
  165.6 5.4 %fusion.54 = bf16[4,512,4,128]{3,1,0,2:T(8,128)(2,1)} fusion(bf16[4,512,4,128]{3,1,0,2:T(8,128)(2,1)} %get-tuple-element.168, s32[]{:T(128)} %get-tuple-element.167, f32[512,4,2048]{2,0,1:T(8,128)S(1)} %get-tuple-element.152, f32[4,512]{1,0:T(4,128)S(1)} %get-tuple-element.153, pred[512,2048]{1,0:T(8,128)(4,1)S(1)} %fusion.52, ...), kind=kOutput, calls=%fused_computation.14.clone.1 | convolution fusion | flops 1091043328 | bytes 18891264 | tf_op jit(solution)/shard_map/while/body/eval_jaxpr/hqk,ke->qhe/dot_general | solution.py:55
  177.0 3.5 %all-to-all-start.4 = ((bf16[4,2,2,128,128]{4,3,2,1,0:T(8,128)(2,1)}), bf16[4,2,2,128,128]{4,3,2,1,0:T(8,128)(2,1)S(1)}, u32[]{:S(2)}, u32[]{:S(2)}) async-start(bf16[4,2,2,128,128]{4,3,2,1,0:T(8,128)(2,1)} %bitcast.50), calls=%async_computation.4 | async-start | bytes 1048576 | tf_op jit(solution)/shard_map/all_to_all | solution.py:102
  183.8 5.5 %all-to-all-done.4 = bf16[4,2,2,128,128]{4,3,2,1,0:T(8,128)(2,1)S(1)} async-done(((bf16[4,2,2,128,128]{4,3,2,1,0:T(8,128)(2,1)}), bf16[4,2,2,128,128]{4,3,2,1,0:T(8,128)(2,1)S(1)}, u32[]{:S(2)}, u32[]{:S(2)}) %all-to-all-start.4) | async-done | bytes 524320 | tf_op jit(solution)/shard_map/all_to_all | solution.py:102
  189.3 3.6 %all-to-all-start.3 = ((bf16[8,256,1,4,128]{4,1,3,2,0:T(8,128)(2,1)}), bf16[8,256,1,4,128]{4,1,3,2,0:T(8,128)(2,1)S(1)}, u32[]{:S(2)}, u32[]{:S(2)}) async-start(bf16[8,256,1,4,128]{4,1,3,2,0:T(8,128)(2,1)} %copy-done), calls=%async_computation.3 | async-start | bytes 4194304 | tf_op jit(solution)/shard_map/all_to_all | solution.py:66
  193.5 47.5 %all-to-all-done.3 = bf16[8,256,1,4,128]{4,1,3,2,0:T(8,128)(2,1)S(1)} async-done(((bf16[8,256,1,4,128]{4,1,3,2,0:T(8,128)(2,1)}), bf16[8,256,1,4,128]{4,1,3,2,0:T(8,128)(2,1)S(1)}, u32[]{:S(2)}, u32[]{:S(2)}) %all-to-all-start.3) | async-done | bytes 2097184 | tf_op jit(solution)/shard_map/all_to_all | solution.py:66
  243.6 4.1 %copy.62 = bf16[1,256,4096]{2,1,0:T(8,128)(2,1)} copy(bf16[1,256,4096]{1,2,0:T(8,128)(2,1)} %bitcast.142) | data formatting | bytes 4194304
  (75 shorter events, 43.2 us)
Async XLA Ops:
  3.1 13.7 %all-to-all-start = ((bf16[8,2,128]{2,1,0:T(2,128)(2,1)}), bf16[8,2,128]{2,1,0:T(2,128)(2,1)S(1)}, u32[]{:S(2)}, u32[]{:S(2)}) async-start(bf16[8,2,128]{2,1,0:T(2,128)(2,1)} %reshape.92), calls=%async_computation | async-start | bytes 8192 | tf_op jit(solution)/shard_map/all_to_all | solution.py:27
  18.0 28.3 %all-to-all-start.2 = ((bf16[256,8,2,128]{3,0,2,1:T(8,128)(2,1)}), bf16[256,8,2,128]{3,0,2,1:T(8,128)(2,1)S(1)}, u32[]{:S(2)}, u32[]{:S(2)}) async-start(bf16[256,8,2,128]{3,0,2,1:T(8,128)(2,1)} %bitcast.6), calls=%async_computation.2 | async-start | bytes 2097152 | tf_op jit(solution)/shard_map/all_to_all | solution.py:26
  27.3 22.7 %copy-start.1 = (bf16[1,256,512]{2,1,0:T(8,128)(2,1)S(1)}, bf16[1,256,512]{2,1,0:T(8,128)(2,1)}, u32[]{:S(2)}) copy-start(bf16[1,256,512]{2,1,0:T(8,128)(2,1)} %param.8) | copy-start | bytes 786436
  46.3 51.9 %all-to-all-start.1 = ((bf16[256,8,4,128]{3,0,2,1:T(8,128)(2,1)}), bf16[256,8,4,128]{3,0,2,1:T(8,128)(2,1)S(1)}, u32[]{:S(2)}, u32[]{:S(2)}) async-start(bf16[256,8,4,128]{3,0,2,1:T(8,128)(2,1)} %copy.51), calls=%async_computation.1 | async-start | bytes 4194304 | tf_op jit(solution)/shard_map/all_to_all | solution.py:36
  50.7 2.5 %copy-start.2 = (s32[1,8,1]{1,2,0:T(1,128)S(1)}, s32[1,8,1]{1,2,0:T(1,128)}, u32[]{:S(2)}) copy-start(s32[1,8,1]{1,2,0:T(1,128)} %param.11) | copy-start | bytes 100
  98.2 78.8 %all-to-all-start.5 = ((bf16[4,2,2]{1,2,0:T(2,128)(2,1)}), bf16[4,2,2]{1,2,0:T(2,128)(2,1)S(1)}, u32[]{:S(2)}, u32[]{:S(2)}) async-start(bf16[4,2,2]{1,2,0:T(2,128)(2,1)} %copy.60), calls=%async_computation.5 | async-start | bytes 4096 | tf_op jit(solution)/shard_map/all_to_all | solution.py:103
  177.0 12.3 %all-to-all-start.4 = ((bf16[4,2,2,128,128]{4,3,2,1,0:T(8,128)(2,1)}), bf16[4,2,2,128,128]{4,3,2,1,0:T(8,128)(2,1)S(1)}, u32[]{:S(2)}, u32[]{:S(2)}) async-start(bf16[4,2,2,128,128]{4,3,2,1,0:T(8,128)(2,1)} %bitcast.50), calls=%async_computation.4 | async-start | bytes 1048576 | tf_op jit(solution)/shard_map/all_to_all | solution.py:102
  182.5 1.3 copy-start
  189.3 51.8 %all-to-all-start.3 = ((bf16[8,256,1,4,128]{4,1,3,2,0:T(8,128)(2,1)}), bf16[8,256,1,4,128]{4,1,3,2,0:T(8,128)(2,1)S(1)}, u32[]{:S(2)}, u32[]{:S(2)}) async-start(bf16[8,256,1,4,128]{4,1,3,2,0:T(8,128)(2,1)} %copy-done), calls=%async_computation.3 | async-start | bytes 4194304 | tf_op jit(solution)/shard_map/all_to_all | solution.py:66
